TPU v7x, 512 devices: a whole 4x4x16 slice. The times are simulated.
512 devices in a mesh: gy: 16 (over x_hi, y, core), gx: 32 (over z, x_lo).
Axes of the slice: x: 4 (x_hi: 2, x_lo: 2; x = x_hi * 2 + x_lo), y: 4, z: 16, core: 2. Of those that a mesh axis runs over, the one named last changes fastest.
Arguments:
- embeddings: bfloat16 [128, 4096, 128], P('gy', 'gx'), may hold values from -180 to 180
- affinity: float32 [4, 128, 4096], P(None, 'gy', 'gx'), may hold values from 0 to 1, as said below
- assignment: int32 [128, 4096], P('gy', 'gx'), may hold values from 0 to 1023
Outputs:
- min_distance: float32 [128, 4096], P('gy', 'gx')
- new_centroids: float32 [1024, 128], replicated
Inputs may be any that keep to these rules, and one draw needn't show every extreme that they name: `affinity`: weight 0 exactly for edges that leave the slab; every other edge weighs 0.05 or more.
All inputs are finite; a program needn't handle non-finite values.
Results may differ from a plain program's by a relative error of at most 0.00045.
Values may be sent and summed in bfloat16 or wider, within the bound.
No kernel may reach another device: no remote copies, remote signals or barrier semaphores. Data moves between devices by JAX's collectives and lax.ppermute only.
A program may use at most 64 MiB of HBM per device.

v0:
```python
import math
import jax
import jax.numpy as jnp
from jax import lax
from jax.sharding import PartitionSpec as P

K = 1024
DEGREE = 4
COEFFS = (0.5, 0.45, 0.35, 0.25, 0.15)


def extended(block, sides, width):
    for axis, dim in sides:
        count = lax.axis_size(axis)
        forward = [(i, i + 1) for i in range(count - 1)]
        backward = [(target, source) for source, target in forward]
        low = lax.ppermute(
            lax.slice_in_dim(block, block.shape[dim] - width, None, axis=dim), axis, forward
        )
        high = lax.ppermute(lax.slice_in_dim(block, 0, width, axis=dim), axis, backward)
        block = jnp.concatenate([low, block, high], axis=dim)
    return block


def degree_of(w_ext):
    w_east, w_south, w_diag, w_anti = (w_ext[0], w_ext[1], w_ext[2], w_ext[3])
    result = w_east[1:-1, 1:-1] + w_east[1:-1, :-2]
    result = result + w_south[1:-1, 1:-1] + w_south[:-2, 1:-1]
    result = result + w_diag[1:-1, 1:-1] + w_diag[:-2, :-2]
    return result + w_anti[1:-1, 1:-1] + w_anti[:-2, 2:]


def edge_sum(w_ext, field):
    w_east, w_south, w_diag, w_anti = (w_ext[0], w_ext[1], w_ext[2], w_ext[3])
    result = w_east[1:-1, 1:-1, None] * field[1:-1, 2:]
    result = result + w_east[1:-1, :-2, None] * field[1:-1, :-2]
    result = result + w_south[1:-1, 1:-1, None] * field[2:, 1:-1]
    result = result + w_south[:-2, 1:-1, None] * field[:-2, 1:-1]
    result = result + w_diag[1:-1, 1:-1, None] * field[2:, 2:]
    result = result + w_diag[:-2, :-2, None] * field[:-2, :-2]
    result = result + w_anti[1:-1, 1:-1, None] * field[2:, :-2]
    return result + w_anti[:-2, 2:, None] * field[:-2, 2:]


def whitening(gram, count):
    lower = jnp.linalg.cholesky(gram)
    identity = jnp.eye(gram.shape[0], dtype=gram.dtype)
    inverse = jax.scipy.linalg.solve_triangular(lower, identity, lower=True)
    return math.sqrt(count) * inverse.T


def on_device(embeddings, affinity, assignment):
    rows, cols, chans = embeddings.shape
    reach_all = DEGREE
    w_width = 1
    w_ext = extended(affinity, (("gy", 1), ("gx", 2)), w_width)
    scale = lax.rsqrt(degree_of(w_ext))[..., None]

    def apply_each(field):
        padded = extended(scale * field, (("gy", 0), ("gx", 1)), 1)
        return scale * edge_sum(w_ext, padded)

    previous = embeddings.astype(jnp.float32)
    current = apply_each(previous)
    filtered = COEFFS[0] * previous + COEFFS[1] * current
    for order in range(2, reach_all + 1):
        following = 2.0 * apply_each(current) - previous
        previous, current = (current, following)
        filtered = filtered + COEFFS[order] * following
    pixels = rows * cols
    flat = filtered.reshape(pixels, chans)
    labels = assignment.reshape(pixels)
    total_pixels = pixels * lax.axis_size("gy") * lax.axis_size("gx")
    clusters = K
    block = 128
    highest = lax.Precision.HIGHEST
    gram_local = lax.dot_general(
        flat, flat, (((0,), (0,)), ((), ())), precision=highest, preferred_element_type=jnp.float32
    )
    gram = lax.psum(gram_local, ("gy", "gx"))
    transform = whitening(gram, total_pixels)
    whitened = jnp.dot(flat, transform, precision=highest, preferred_element_type=jnp.float32)

    def one_block(index):
        first = index * block
        onehot = (labels[:, None] == first + jnp.arange(block, dtype=jnp.int32)[None, :]).astype(
            jnp.float32
        )
        partial_sums = lax.dot_general(
            onehot,
            whitened,
            (((0,), (0,)), ((), ())),
            precision=highest,
            preferred_element_type=jnp.float32,
        )
        return (partial_sums, jnp.sum(onehot, axis=0))

    block_sums, block_counts = lax.map(one_block, jnp.arange(clusters // block, dtype=jnp.int32))
    local_sums = block_sums.reshape(clusters, chans)
    local_counts = block_counts.reshape(clusters)
    sums, counts = lax.psum((local_sums, local_counts), ("gy", "gx"))
    centroids = sums / (counts + 1.0)[:, None]
    norms = jnp.sum(whitened * whitened, axis=1)

    def nearest(index, best):
        centre_part = lax.dynamic_slice_in_dim(centroids, index * block, block, 0)
        cross = lax.dot_general(
            whitened,
            centre_part,
            (((1,), (1,)), ((), ())),
            precision=highest,
            preferred_element_type=jnp.float32,
        )
        part_norms = jnp.sum(centre_part * centre_part, axis=1)
        distance = (norms[:, None] - 2.0 * cross + part_norms[None, :]) / chans
        return jnp.minimum(best, jnp.min(distance, axis=1))

    best = lax.fori_loop(0, clusters // block, nearest, jnp.full((pixels,), jnp.inf, jnp.float32))
    return (best.reshape(rows, cols), centroids)


def solution(mesh):
    return jax.shard_map(
        on_device,
        mesh=mesh,
        in_specs=(P("gy", "gx", None), P(None, "gy", "gx"), P("gy", "gx")),
        out_specs=(P("gy", "gx"), P()),
        check_vma=False,
    )
```

profile of v0, /device:TPU:4, one launch (start us, length us, event | category | flops | bytes accessed | tf_op | source)
XLA Modules:
  0.0 1084.3 jit_solution(14910961055857017236)
XLA Ops:
  8.0 2.0 collective-permute-start
  10.1 7.4 collective-permute-start.1
  19.6 3.1 collective-permute-start.2
  22.7 1.3 collective-permute-start.3
  24.2 4.4 collective-permute-done.3
  29.1 1.9 collective-permute-start.4
  31.0 7.3 collective-permute-start.5
  38.3 1.9 collective-permute-done.5
  40.2 1.3 collective-permute-start.6
  41.5 5.4 collective-permute-start.7
  46.9 1.3 collective-permute-done.7
  48.3 1.7 broadcast_multiply_fusion.2
  50.1 1.9 collective-permute-start.8
  52.0 7.3 collective-permute-start.9
  59.3 1.9 collective-permute-done.9
  61.2 1.3 collective-permute-start.10
  62.5 5.4 collective-permute-start.11
  67.9 1.3 collective-permute-done.11
  69.3 1.7 broadcast_multiply_fusion.1
  71.0 1.9 collective-permute-start.12
  73.0 7.3 collective-permute-start.13
  80.2 1.9 collective-permute-done.13
  83.4 5.7 collective-permute-start.15
  89.2 1.3 collective-permute-done.15
  90.6 1.7 broadcast_multiply_fusion
  92.3 1.9 collective-permute-start.16
  94.3 7.3 collective-permute-start.17
  101.5 1.9 collective-permute-done.17
  103.4 1.3 collective-permute-start.18
  104.7 5.7 collective-permute-start.19
  110.5 1.3 collective-permute-done.19
  111.9 1.7 fusion.14
  113.6 1.6 convolution_bitcast_fusion.1
  115.5 453.4 %all-reduce.3.cloned.1.call-done = f32[128,128]{0,1:T(8,128)} async-done(((f32[128,128]{0,1:T(8,128)}), f32[128,128]{0,1:T(8,128)}) %all-reduce.3.cloned.1.call-update) | async-done | bytes 65552 | tf_op jit(solution)/shard_map/psum | solution.py:80
  569.9 11.7 %cholesky.14 = f32[128,128]{1,0:T(8,128)S(1)} custom-call(f32[128,128]{1,0:T(8,128)S(1)} %fusion.63), custom_call_target="Cholesky" | custom-call | tf_op jit(solution)/shard_map/jit(cholesky)/cholesky | solution.py:46
  582.9 9.8 custom-call.7
  594.3 23.2 %while.26 = (s32[]{:T(128)}, f32[8,128,128]{2,1,0:T(8,128)}, f32[8,128]{1,0:T(8,128)S(1)}, s32[8,128]{1,0:T(8,128)S(1)}, s32[8]{0:T(128)S(1)}, /*index=5*/f32[10...) while((s32[]{:T(128)}, f32[8,128,128]{2,1,0:T(8,128)}, f32[8,128]{1,0:T(8,128)S(1)}, ...), condition=%wide.region_5.6_spmd, body=%wide.region_3.5_spmd.sunk | while | flops 201850880 | bytes 601725 | solution.py:98
  595.6 1.4 fusion.88
  598.5 1.4 fusion.88
  601.4 1.4 fusion.88
  604.3 1.4 fusion.88
  607.2 1.4 fusion.88
  610.1 1.4 fusion.88
  613.0 1.4 fusion.88
  615.9 1.4 fusion.88
  617.6 101.1 %psum.23 = f32[1024]{0:T(1024)S(1)} all-reduce(f32[1024]{0:T(1024)S(1)} %bitcast.54), channel_id=1, replica_groups=mesh['gy'=16,'gx'=32] {'gy','gx'}, use_global_device_ids=true, to_apply=%region_7.8 | all-reduce | flops 1024 | bytes 8192 | tf_op jit(solution)/shard_map/psum | solution.py:101
  718.7 350.4 %all-reduce.5.cloned.1.call-done = f32[1024,128]{1,0:T(8,128)} async-done(((f32[1024,128]{1,0:T(8,128)}), f32[1024,128]{1,0:T(8,128)}) %all-reduce.5.cloned.1.call-update) | async-done | bytes 524304 | tf_op jit(solution)/shard_map/psum | solution.py:101
  1070.3 6.3 while.27
  (117 shorter events, 24.3 us)
Async XLA Ops:
  7.2 561.7 %all-reduce.3.cloned.1.call-start = ((), (), s32[]{:S(2)}) async-start(), calls=%async_computation | async-start | bytes 131072 | tf_op jit(solution)/shard_map/psum | solution.py:80
  8.0 20.6 %copy-start.5 = (f32[4,8,128]{2,1,0:T(8,128)S(1)}, f32[4,8,128]{2,1,0:T(8,128)}, u32[]{:S(2)}) copy-start(f32[4,8,128]{2,1,0:T(8,128)} %param.8) | copy-start | bytes 49156
  8.0 9.5 collective-permute-start
  10.1 18.8 %copy-start = (bf16[8,128,128]{2,1,0:T(8,128)(2,1)S(1)}, bf16[8,128,128]{2,1,0:T(8,128)(2,1)}, u32[]{:S(2)}) copy-start(bf16[8,128,128]{2,1,0:T(8,128)(2,1)} %param.7) | copy-start | bytes 786436
  10.1 8.7 collective-permute-start.1
  19.6 4.7 collective-permute-start.2
  22.7 6.0 collective-permute-start.3
  29.1 9.2 collective-permute-start.4
  31.0 9.1 collective-permute-start.5
  40.2 6.8 collective-permute-start.6
  41.5 6.8 collective-permute-start.7
  50.1 9.2 collective-permute-start.8
  52.0 9.1 collective-permute-start.9
  61.2 6.8 collective-permute-start.10
  62.5 6.8 collective-permute-start.11
  71.0 9.2 collective-permute-start.12
  73.0 9.1 collective-permute-start.13
  82.1 7.0 collective-permute-start.14
  83.4 7.0 collective-permute-start.15
  92.3 9.2 collective-permute-start.16
  94.3 9.1 collective-permute-start.17
  103.4 7.0 collective-permute-start.18
  104.7 7.0 collective-permute-start.19
  115.2 953.8 %all-reduce.5.cloned.1.call-start = ((), (), s32[]{:S(2)}) async-start(), calls=%async_computation.1 | async-start | bytes 1048576 | tf_op jit(solution)/shard_map/psum | solution.py:101
  568.8 1.0 copy-start.3
  593.6 0.7 copy-start.2
  1076.6 0.8 copy-start.1
  1076.7 0.8 copy-start.4
Sparse Core Ops, SparseCore 0:
  115.3 453.4 all-reduce.2
  617.7 451.3 all-reduce.4
where the time goes:
time: 1090 us; the launch traced here: 1080 us
  waiting for transfers between devices  823 us (76%)
  blocking collectives  101 us (9%)
  starting transfers between devices  78.3 us (7%)
  other arithmetic  35.1 us (3%)
  matrix products  18.7 us (2%)
  between operations  14.5 us (1%)
    psum x1, waiting for transfers between devices, on_device(): gram = lax.psum(gram_local, ('gy', 'gx'))  453 us
    psum x1, waiting for transfers between devices, on_device(): sums, counts = lax.psum((local_sums, local_counts), ('gy', 'gx'))  350 us
    psum x1, blocking collectives, on_device(): sums, counts = lax.psum((local_sums, local_counts), ('gy', 'gx'))  101 us
    ppermute x10, starting transfers between devices, extended(): lax.ppermute(lax.slice_in_dim(block, 0, width, axis=dim), axis, backward)  42.9 us
    ppermute x10, starting transfers between devices, extended(): lax.ppermute(lax.slice_in_dim(block, block.shape[dim] - width, None, axis...  35.1 us
  transfers between devices with their start and end apart: 22, of which 13 were waited for; matrix products, arithmetic and copies ran while one was open for 0% of the time, Pallas kernels for 0%

commit v1 on v0

--- a/solution.py
+++ b/solution.py
@@ -77,7 +77,7 @@
     gram_local = lax.dot_general(
         flat, flat, (((0,), (0,)), ((), ())), precision=highest, preferred_element_type=jnp.float32
     )
-    gram = lax.psum(gram_local, ("gy", "gx"))
+    gram = jnp.sum(lax.all_gather(gram_local, ("gy", "gx")), axis=0)
     transform = whitening(gram, total_pixels)
     whitened = jnp.dot(flat, transform, precision=highest, preferred_element_type=jnp.float32)
 

time: 1090 us -> 2130 us (1.95)
  waiting for transfers between devices: 823 us -> 1840 us
    all_gather x0 -> x1, waiting for transfers between devices: none -> 1470 us  [on_device(): gram = jnp.sum(lax.all_gather(gram_local, ('gy', 'gx')), axis=0)]
    psum x1 -> x0, waiting for transfers between devices: 453 us -> none  [on_device(): gram = lax.psum(gram_local, ('gy', 'gx'))]
where the time goes in v1:
time: 2130 us
  waiting for transfers between devices  1840 us (86%)
  blocking collectives  110 us (5%)
  starting transfers between devices  78 us (4%)
  other arithmetic  52.4 us (2%)
    all_gather x1, waiting for transfers between devices, on_device(): gram = jnp.sum(lax.all_gather(gram_local, ('gy', 'gx')), axis=0)  1470 us
    psum x1, waiting for transfers between devices, on_device(): sums, counts = lax.psum((local_sums, local_counts), ('gy', 'gx'))  355 us
    psum x1, blocking collectives, on_device(): sums, counts = lax.psum((local_sums, local_counts), ('gy', 'gx'))  110 us
    ppermute x10, starting transfers between devices, extended(): lax.ppermute(lax.slice_in_dim(block, 0, width, axis=dim), axis, backward)  42.7 us
  transfers between devices with their start and end apart: 22, of which 13 were waited for; matrix products, arithmetic and copies ran while one was open for 0% of the time, Pallas kernels for 0%

profile of v1, /device:TPU:4, one launch (start us, length us, event | category | flops | bytes accessed | tf_op | source)
XLA Modules:
  0.0 2130.6 jit_solution(1593534954685747406)
XLA Ops:
  8.0 1.9 collective-permute-start
  9.9 7.3 collective-permute-start.1
  19.3 3.1 collective-permute-start.2
  22.4 1.3 collective-permute-start.3
  24.0 4.4 collective-permute-done.3
  30.5 1.9 collective-permute-start.4
  32.4 7.3 collective-permute-start.5
  39.7 1.9 collective-permute-done.5
  41.6 1.3 collective-permute-start.6
  42.9 5.4 collective-permute-start.7
  48.3 1.3 collective-permute-done.7
  49.7 1.7 broadcast_multiply_fusion.2
  51.5 1.9 collective-permute-start.8
  53.4 7.3 collective-permute-start.9
  60.7 1.9 collective-permute-done.9
  63.8 5.4 collective-permute-start.11
  69.3 1.3 collective-permute-done.11
  70.7 3.0 broadcast_multiply_fusion.1
  73.7 1.9 collective-permute-start.12
  75.6 7.3 collective-permute-start.13
  82.9 1.9 collective-permute-done.13
  86.1 5.7 collective-permute-start.15
  91.8 1.3 collective-permute-done.15
  93.2 1.7 broadcast_multiply_fusion
  95.0 1.9 collective-permute-start.16
  96.9 7.3 collective-permute-start.17
  104.2 1.9 collective-permute-done.17
  106.1 1.3 collective-permute-start.18
  107.4 5.7 collective-permute-start.19
  113.1 1.3 collective-permute-done.19
  114.5 3.0 fusion.14
  117.5 1.6 convolution_bitcast_fusion.1
  119.4 1470.5 %all-gather.3.cloned.1.call-done = f32[65536,128]{1,0:T(8,128)} async-done(((f32[128,128]{1,0:T(8,128)}), f32[65536,128]{1,0:T(8,128)}) %all-gather.3.cloned.1.call-update) | async-done | bytes 33554448 | tf_op jit(solution)/shard_map/all_gather | solution.py:80
  1589.9 13.1 reduce_sum.40
  1603.1 11.7 cholesky.14
  1616.2 9.8 custom-call.7
  1627.1 23.2 %while.26 = (s32[]{:T(128)}, f32[8,128,128]{2,1,0:T(8,128)}, f32[8,128]{1,0:T(8,128)S(1)}, s32[8,128]{1,0:T(8,128)S(1)}, s32[8]{0:T(128)S(1)}, /*index=5*/f32[10...) while((s32[]{:T(128)}, f32[8,128,128]{2,1,0:T(8,128)}, f32[8,128]{1,0:T(8,128)S(1)}, ...), condition=%wide.region_5.6_spmd, body=%wide.region_3.5_spmd.sunk | while | flops 201850880 | bytes 601725 | solution.py:98
  1628.3 1.4 fusion.88
  1631.2 1.4 fusion.88
  1634.1 1.4 fusion.88
  1637.0 1.4 fusion.88
  1639.9 1.4 fusion.88
  1642.8 1.4 fusion.88
  1645.7 1.4 fusion.88
  1648.6 1.4 fusion.88
  1650.3 110.5 %psum.15 = f32[1024]{0:T(1024)S(1)} all-reduce(f32[1024]{0:T(1024)S(1)} %bitcast.56), channel_id=1, replica_groups=mesh['gy'=16,'gx'=32] {'gy','gx'}, use_global_device_ids=true, to_apply=%region_7.8 | all-reduce | flops 1024 | bytes 8192 | tf_op jit(solution)/shard_map/psum | solution.py:101
  1760.8 354.5 %all-reduce.2.cloned.1.call-done = f32[1024,128]{1,0:T(8,128)} async-done(((f32[1024,128]{1,0:T(8,128)}), f32[1024,128]{1,0:T(8,128)}) %all-reduce.2.cloned.1.call-update) | async-done | bytes 524304 | tf_op jit(solution)/shard_map/psum | solution.py:101
  2116.6 6.4 while.27
  (112 shorter events, 25.9 us)
Async XLA Ops:
  7.2 1582.7 %all-gather.3.cloned.1.call-start = ((), (), s32[]{:S(2)}) async-start(), calls=%async_computation.1 | async-start | bytes 33619968 | tf_op jit(solution)/shard_map/all_gather | solution.py:80
  8.0 9.2 collective-permute-start
  9.9 8.6 collective-permute-start.1
  19.3 4.7 collective-permute-start.2
  22.4 6.0 collective-permute-start.3
  30.5 9.2 collective-permute-start.4
  32.4 9.1 collective-permute-start.5
  41.6 6.8 collective-permute-start.6
  42.9 6.8 collective-permute-start.7
  49.7 1577.3 %copy-start.1 = (s32[8,128]{1,0:T(8,128)S(1)}, s32[8,128]{1,0:T(8,128)}, u32[]{:S(2)}) copy-start(s32[8,128]{1,0:T(8,128)} %param.9) | copy-start | bytes 12292
  51.5 9.2 collective-permute-start.8
  53.4 9.1 collective-permute-start.9
  62.5 6.8 collective-permute-start.10
  63.8 6.8 collective-permute-start.11
  73.7 9.2 collective-permute-start.12
  75.6 9.1 collective-permute-start.13
  84.8 7.0 collective-permute-start.14
  86.1 7.0 collective-permute-start.15
  95.0 9.2 collective-permute-start.16
  96.9 9.1 collective-permute-start.17
  106.1 7.0 collective-permute-start.18
  107.4 7.0 collective-permute-start.19
  119.2 1996.2 %all-reduce.2.cloned.1.call-start = ((), (), s32[]{:S(2)}) async-start(), calls=%async_computation | async-start | bytes 1048576 | tf_op jit(solution)/shard_map/psum | solution.py:101
  2123.0 0.8 copy-start
  2123.0 0.8 copy-start.2
Sparse Core Ops, SparseCore 0:
  119.3 1470.5 all-gather.2
  1650.4 464.8 all-reduce.1
